TPU v7x, 32 devices: a whole 2x2x4 slice. The times are simulated.
32 devices in a mesh: rep: 4 (over y, x), fsdp: 8 (over z, core).
Axes of the slice: x: 2, y: 2, z: 4, core: 2. Of those that a mesh axis runs over, the one named last changes fastest.
Arguments:
- tokens: float32 [4096, 1024], P(('rep', 'fsdp')), may hold values from -6 to 6
- segment_ids: int32 [4096], replicated, may hold values from 0 to 7, never falling along the last dimension, each value on 1 to 1024 neighbouring positions
- cotangent: float32 [4096, 1024], P(('rep', 'fsdp')), may hold values from -6 to 6
- w_qkv: bfloat16 [1024, 2048], P('fsdp'), may hold values from -0.1875 to 0.1875
- w_out: bfloat16 [1024, 1024], P('fsdp'), may hold values from -0.75 to 0.75
- w_gate_up: bfloat16 [1024, 9216], P('fsdp'), may hold values from -0.1875 to 0.1875
- w_down: bfloat16 [4608, 1024], P('fsdp'), may hold values from -0.09375 to 0.09375
- g_attn: bfloat16 [1024], P('fsdp'), may hold values from 0.099609375 to 1.8984375
- g_query: bfloat16 [64], P('fsdp'), may hold values from 0.099609375 to 1.8984375
- g_key: bfloat16 [64], P('fsdp'), may hold values from 0.099609375 to 1.8984375
- g_ffn: bfloat16 [1024], P('fsdp'), may hold values from 0.099609375 to 1.8984375
Outputs:
- output: float32 [4096, 1024], P(('rep', 'fsdp'))
- grad_tokens: float32 [4096, 1024], P(('rep', 'fsdp'))
- grad_w_qkv: float32 [1024, 2048], P('fsdp')
- grad_w_out: float32 [1024, 1024], P('fsdp')
- grad_w_gate_up: float32 [1024, 9216], P('fsdp')
- grad_w_down: float32 [4608, 1024], P('fsdp')
- grad_g_attn: float32 [1024], P('fsdp')
- grad_g_query: float32 [64], P('fsdp')
- grad_g_key: float32 [64], P('fsdp')
- grad_g_ffn: float32 [1024], P('fsdp')
Inputs may be any that keep to these rules, and one draw needn't show every extreme that they name: `segment_ids`: segment numbers never fall along the tokens; a segment holds 1 to 1024 tokens and one holds exactly 1024.
All inputs are finite; a program needn't handle non-finite values.
Results may differ from a plain program's by a relative error of at most 0.024.
Values may be sent and summed in bfloat16 or wider, within the bound.
A program may use at most 192 MiB of HBM per device.

v0:
```python
import jax
import jax.numpy as jnp
from jax import lax
from jax.sharding import PartitionSpec as P

QUERY_HEADS = 16
KEY_VALUE_HEADS = 8
HEAD_SIZE = 64
FF = 4608
NORM_EPS = 1e-05
ROPE_BASE = 1000000.0
MASK_FILL = -1e30


def rms_forward(values, gain_vec):
    inv_rms = lax.rsqrt(jnp.mean(values * values, axis=-1, keepdims=True) + NORM_EPS)
    return (values * inv_rms * gain_vec, inv_rms)


def root_mean_square_reverse(values, inv_rms, gain_vec, grad_out):
    weighted = grad_out * gain_vec
    grad_values = inv_rms * weighted - values * inv_rms**3 * jnp.mean(
        weighted * values, axis=-1, keepdims=True
    )
    grad_gain = jnp.sum((grad_out * values * inv_rms).reshape(-1, values.shape[-1]), axis=0)
    return (grad_values, grad_gain)


def rope_tables(positions, head_width):
    half_width = head_width // 2
    freqs_base = ROPE_BASE ** (-2.0 * jnp.arange(half_width, dtype=jnp.float32) / head_width)
    angles = positions.astype(jnp.float32)[:, None] * freqs_base[None, :]
    return (jnp.cos(angles)[:, None, :], jnp.sin(angles)[:, None, :])


def rotary_embed_apply(values, rotary_cosine, rotary_sine):
    half_width = values.shape[-1] // 2
    first_half = values[..., :half_width]
    second_half = values[..., half_width:]
    return jnp.concatenate(
        [
            first_half * rotary_cosine - second_half * rotary_sine,
            second_half * rotary_cosine + first_half * rotary_sine,
        ],
        axis=-1,
    )


def rotary_embed_invert(grad_out, rotary_cosine, rotary_sine):
    half_width = grad_out.shape[-1] // 2
    first_half = grad_out[..., :half_width]
    second_half = grad_out[..., half_width:]
    return jnp.concatenate(
        [
            first_half * rotary_cosine + second_half * rotary_sine,
            second_half * rotary_cosine - first_half * rotary_sine,
        ],
        axis=-1,
    )


def score_block(query_lowprec, key_lowprec, attention_mask_matrix):
    scale_dot = query_lowprec.shape[-1] ** (-0.5)
    scores = (
        jnp.einsum("qkgd,tkd->kgqt", query_lowprec, key_lowprec, preferred_element_type=jnp.float32)
        * scale_dot
    )
    return jnp.where(attention_mask_matrix, scores, MASK_FILL)


def attend_forward(query_lowprec, key_lowprec, value_lowprec, attention_mask_matrix):
    scores = score_block(query_lowprec, key_lowprec, attention_mask_matrix)
    top_score = jnp.max(scores, axis=-1, keepdims=True)
    expo_terms = jnp.where(attention_mask_matrix, jnp.exp(scores - top_score), 0.0)
    row_total = jnp.sum(expo_terms, axis=-1, keepdims=True)
    probs = (expo_terms / row_total).astype(jnp.bfloat16)
    mixed = jnp.einsum("kgqt,tkd->qkgd", probs, value_lowprec, preferred_element_type=jnp.float32)
    return (mixed.astype(jnp.bfloat16), top_score + jnp.log(row_total))


def attention_reverse_pass(
    query_lowprec,
    key_lowprec,
    value_lowprec,
    attention_mask_matrix,
    attention_lowprec,
    log_partition_sum,
    grad_attn,
):
    scale_dot = query_lowprec.shape[-1] ** (-0.5)
    scores = score_block(query_lowprec, key_lowprec, attention_mask_matrix)
    probs_again = jnp.where(attention_mask_matrix, jnp.exp(scores - log_partition_sum), 0.0)
    probs_low = probs_again.astype(jnp.bfloat16)
    value_gradient_rows = jnp.einsum(
        "kgqt,qkgd->tkd", probs_low, grad_attn, preferred_element_type=jnp.float32
    )
    d_probs = jnp.einsum(
        "qkgd,tkd->kgqt", grad_attn, value_lowprec, preferred_element_type=jnp.float32
    )
    delta_rows = jnp.sum(
        grad_attn.astype(jnp.float32) * attention_lowprec.astype(jnp.float32), axis=-1
    )
    delta_rows = jnp.transpose(delta_rows, (1, 2, 0))[..., None]
    d_score = (probs_again * (d_probs - delta_rows) * scale_dot).astype(jnp.bfloat16)
    grad_query = jnp.einsum(
        "kgqt,tkd->qkgd", d_score, key_lowprec, preferred_element_type=jnp.float32
    )
    grad_key = jnp.einsum(
        "kgqt,qkgd->tkd", d_score, query_lowprec, preferred_element_type=jnp.float32
    )
    return (grad_query, grad_key, value_gradient_rows)


def tdot(left_arr, right_arr):
    return lax.dot_general(
        left_arr, right_arr, (((0,), (0,)), ((), ())), preferred_element_type=jnp.float32
    )


def transposed_product(left_arr, right_arr):
    return lax.dot_general(
        left_arr, right_arr, (((1,), (1,)), ((), ())), preferred_element_type=jnp.float32
    )


def body(
    tokens, segment_ids, cotangent, w_qkv, w_out, w_gate_up, w_down, g_attn, g_query, g_key, g_ffn
):
    local_rows = tokens.shape[0]
    cluster_size = QUERY_HEADS // KEY_VALUE_HEADS
    seq_devices = lax.axis_size("fsdp")
    cluster_rows = seq_devices * local_rows
    member = lax.axis_index("fsdp")
    own_group = member * local_rows
    group_start = lax.axis_index("rep") * cluster_rows
    own_global = group_start + own_group
    key_value_width = KEY_VALUE_HEADS * HEAD_SIZE
    shards = (w_qkv, w_out, w_gate_up, w_down, g_attn, g_query, g_key, g_ffn)
    collected_rows = (
        lax.all_gather(shards[0], "fsdp", axis=0, tiled=True),
        lax.all_gather(shards[1], "fsdp", axis=0, tiled=True),
        lax.all_gather(shards[2], "fsdp", axis=0, tiled=True),
        lax.all_gather(shards[3], "fsdp", axis=0, tiled=True),
        lax.all_gather(shards[4], "fsdp", axis=0, tiled=True),
        lax.all_gather(shards[5], "fsdp", axis=0, tiled=True),
        lax.all_gather(shards[6], "fsdp", axis=0, tiled=True),
        lax.all_gather(shards[7], "fsdp", axis=0, tiled=True),
    )
    gain_sequence = [gain_arr.astype(jnp.float32) for gain_arr in collected_rows[4:]]
    query_seg = lax.dynamic_slice_in_dim(segment_ids, own_global, local_rows)
    key_seg = lax.dynamic_slice_in_dim(segment_ids, group_start, cluster_rows)
    query_pos = own_group + jnp.arange(local_rows, dtype=jnp.int32)
    key_pos = jnp.arange(cluster_rows, dtype=jnp.int32)
    attention_mask_matrix = (key_pos[None, :] <= query_pos[:, None]) & (
        query_seg[:, None] == key_seg[None, :]
    )
    rotary_cosine, rotary_sine = rope_tables(query_pos, HEAD_SIZE)
    normed_f, inv_in = rms_forward(tokens, gain_sequence[0])
    normed_in = normed_f.astype(jnp.bfloat16)
    projection_output = jnp.dot(normed_in, collected_rows[0], preferred_element_type=jnp.float32)
    query_raw = projection_output[:, : QUERY_HEADS * HEAD_SIZE].reshape(
        local_rows, QUERY_HEADS, HEAD_SIZE
    )
    key_unrotated = projection_output[
        :, QUERY_HEADS * HEAD_SIZE : (QUERY_HEADS + KEY_VALUE_HEADS) * HEAD_SIZE
    ].reshape(local_rows, KEY_VALUE_HEADS, HEAD_SIZE)
    value_lowprec = projection_output[:, (QUERY_HEADS + KEY_VALUE_HEADS) * HEAD_SIZE :].astype(
        jnp.bfloat16
    )
    query_norm_output, inv_query = rms_forward(query_raw, gain_sequence[1])
    key_norm, key_inverse_norm = rms_forward(key_unrotated, gain_sequence[2])
    query_lowprec = (
        rotary_embed_apply(query_norm_output, rotary_cosine, rotary_sine)
        .astype(jnp.bfloat16)
        .reshape(local_rows, KEY_VALUE_HEADS, cluster_size, HEAD_SIZE)
    )
    key_lowprec = rotary_embed_apply(key_norm, rotary_cosine, rotary_sine).astype(jnp.bfloat16)
    kv_pair = jnp.stack([key_lowprec.reshape(local_rows, key_value_width), value_lowprec])
    key_value_span = lax.all_gather(kv_pair, "fsdp", axis=1, tiled=True)
    span_keys = key_value_span[0].reshape(cluster_rows, KEY_VALUE_HEADS, HEAD_SIZE)
    span_values = key_value_span[1].reshape(cluster_rows, KEY_VALUE_HEADS, HEAD_SIZE)
    attention_lowprec, log_partition_sum = attend_forward(
        query_lowprec, span_keys, span_values, attention_mask_matrix
    )
    attn_flat = attention_lowprec.reshape(local_rows, QUERY_HEADS * HEAD_SIZE)
    mid_stream = tokens + jnp.dot(attn_flat, collected_rows[1], preferred_element_type=jnp.float32)
    normed_g, inv_mid = rms_forward(mid_stream, gain_sequence[3])
    normed_mid = normed_g.astype(jnp.bfloat16)
    gate_up = jnp.dot(normed_mid, collected_rows[2], preferred_element_type=jnp.float32)
    gate_part = gate_up[:, :FF]
    up_part = gate_up[:, FF:]
    sigmoid_gate = jax.nn.sigmoid(gate_part)
    hidden = (gate_part * sigmoid_gate * up_part).astype(jnp.bfloat16)
    output = mid_stream + jnp.dot(hidden, collected_rows[3], preferred_element_type=jnp.float32)
    cot_low = cotangent.astype(jnp.bfloat16)
    grad_down = tdot(hidden, cot_low)
    d_hidden = transposed_product(cot_low, collected_rows[3])
    d_gate = d_hidden * up_part * sigmoid_gate * (1.0 + gate_part * (1.0 - sigmoid_gate))
    d_up = d_hidden * gate_part * sigmoid_gate
    d_gate_up = jnp.concatenate([d_gate, d_up], axis=1).astype(jnp.bfloat16)
    grad_gate_up = tdot(normed_mid, d_gate_up)
    d_normed_mid = transposed_product(d_gate_up, collected_rows[2])
    back_mid, grad_ffn_gain = root_mean_square_reverse(
        mid_stream, inv_mid, gain_sequence[3], d_normed_mid
    )
    d_mid = cotangent + back_mid
    middle_cotangent_lowprec = d_mid.astype(jnp.bfloat16)
    grad_out_proj = tdot(attn_flat, middle_cotangent_lowprec)
    attention_cotangent = (
        transposed_product(middle_cotangent_lowprec, collected_rows[1])
        .astype(jnp.bfloat16)
        .reshape(local_rows, KEY_VALUE_HEADS, cluster_size, HEAD_SIZE)
    )
    query_lowprec_gradient, grad_kwin, grad_vwin = attention_reverse_pass(
        query_lowprec,
        span_keys,
        span_values,
        attention_mask_matrix,
        attention_lowprec,
        log_partition_sum,
        attention_cotangent,
    )
    kv_grads = jnp.stack(
        [
            grad_kwin.reshape(cluster_rows, key_value_width),
            grad_vwin.reshape(cluster_rows, key_value_width),
        ]
    )
    local_key_value = lax.psum_scatter(
        kv_grads.astype(jnp.bfloat16), "fsdp", scatter_dimension=1, tiled=True
    ).astype(jnp.float32)
    d_query, grad_query_gain = root_mean_square_reverse(
        query_raw,
        inv_query,
        gain_sequence[1],
        rotary_embed_invert(
            query_lowprec_gradient.reshape(local_rows, QUERY_HEADS, HEAD_SIZE),
            rotary_cosine,
            rotary_sine,
        ),
    )
    key_cotangent, key_gain_gradient = root_mean_square_reverse(
        key_unrotated,
        key_inverse_norm,
        gain_sequence[2],
        rotary_embed_invert(
            local_key_value[0].reshape(local_rows, KEY_VALUE_HEADS, HEAD_SIZE),
            rotary_cosine,
            rotary_sine,
        ),
    )
    d_projected = jnp.concatenate(
        [
            d_query.reshape(local_rows, -1),
            key_cotangent.reshape(local_rows, -1),
            local_key_value[1],
        ],
        axis=1,
    ).astype(jnp.bfloat16)
    grad_qkv = tdot(normed_in, d_projected)
    d_normed_in = transposed_product(d_projected, collected_rows[0])
    back_in, grad_attn_gain = root_mean_square_reverse(
        tokens, inv_in, gain_sequence[0], d_normed_in
    )
    grad_tokens = d_mid + back_in
    grads_local = (
        grad_qkv,
        grad_out_proj,
        grad_gate_up,
        grad_down,
        grad_attn_gain,
        grad_query_gain,
        key_gain_gradient,
        grad_ffn_gain,
    )
    grad_share = (
        lax.psum_scatter(
            grads_local[0].astype(jnp.bfloat16), "fsdp", scatter_dimension=0, tiled=True
        ).astype(jnp.float32),
        lax.psum_scatter(
            grads_local[1].astype(jnp.bfloat16), "fsdp", scatter_dimension=0, tiled=True
        ).astype(jnp.float32),
        lax.psum_scatter(
            grads_local[2].astype(jnp.bfloat16), "fsdp", scatter_dimension=0, tiled=True
        ).astype(jnp.float32),
        lax.psum_scatter(
            grads_local[3].astype(jnp.bfloat16), "fsdp", scatter_dimension=0, tiled=True
        ).astype(jnp.float32),
        lax.psum_scatter(
            grads_local[4].astype(jnp.bfloat16), "fsdp", scatter_dimension=0, tiled=True
        ).astype(jnp.float32),
        lax.psum_scatter(
            grads_local[5].astype(jnp.bfloat16), "fsdp", scatter_dimension=0, tiled=True
        ).astype(jnp.float32),
        lax.psum_scatter(
            grads_local[6].astype(jnp.bfloat16), "fsdp", scatter_dimension=0, tiled=True
        ).astype(jnp.float32),
        lax.psum_scatter(
            grads_local[7].astype(jnp.bfloat16), "fsdp", scatter_dimension=0, tiled=True
        ).astype(jnp.float32),
    )
    grad_total = (
        lax.psum(grad_share[0].astype(jnp.bfloat16), "rep").astype(jnp.float32),
        lax.psum(grad_share[1].astype(jnp.bfloat16), "rep").astype(jnp.float32),
        lax.psum(grad_share[2].astype(jnp.bfloat16), "rep").astype(jnp.float32),
        lax.psum(grad_share[3].astype(jnp.bfloat16), "rep").astype(jnp.float32),
        lax.psum(grad_share[4].astype(jnp.bfloat16), "rep").astype(jnp.float32),
        lax.psum(grad_share[5].astype(jnp.bfloat16), "rep").astype(jnp.float32),
        lax.psum(grad_share[6].astype(jnp.bfloat16), "rep").astype(jnp.float32),
        lax.psum(grad_share[7].astype(jnp.bfloat16), "rep").astype(jnp.float32),
    )
    return (
        output,
        grad_tokens,
        grad_total[0],
        grad_total[1],
        grad_total[2],
        grad_total[3],
        grad_total[4],
        grad_total[5],
        grad_total[6],
        grad_total[7],
    )


def solution(mesh):
    placed = (
        P(("rep", "fsdp"), None),
        P(),
        P(("rep", "fsdp"), None),
        P("fsdp", None),
        P("fsdp", None),
        P("fsdp", None),
        P("fsdp", None),
        P("fsdp"),
        P("fsdp"),
        P("fsdp"),
        P("fsdp"),
    )
    return jax.shard_map(
        body,
        mesh=mesh,
        in_specs=placed,
        out_specs=(
            P(("rep", "fsdp"), None),
            P(("rep", "fsdp"), None),
            P("fsdp", None),
            P("fsdp", None),
            P("fsdp", None),
            P("fsdp", None),
            P("fsdp"),
            P("fsdp"),
            P("fsdp"),
            P("fsdp"),
        ),
        check_vma=False,
    )
```

profile of v0, /device:TPU:0, one launch (start us, length us, event | category | flops | bytes accessed | tf_op | source)
XLA Modules:
  0.0 968.5 jit_solution(10914518348454304523)
XLA Ops:
  8.0 13.6 %all-gather = bf16[8,1,128]{2,1,0:T(2,128)(2,1)S(1)} all-gather(bf16[1,1,128]{2,1,0:T(2,128)(2,1)} %bitcast.157), channel_id=1, replica_groups=mesh['rep'=4,'fsdp'=8] {'fsdp'}, dimensions={0}, use_global_device_ids=true | all-gather | bytes 2304 | tf_op jit(solution)/shard_map/all_gather | solution.py:144
  25.3 15.0 %all-reduce.7 = (bf16[64]{0:T(256)(128)(2,1)S(1)}, bf16[64]{0:T(256)(128)(2,1)S(1)}) all-reduce(bf16[64]{0:T(256)(128)(2,1)S(1)} %dynamic-update-slice, bf16[64]{0:T(256)(128)(2,1)S(1)} %dynamic-update-slice.1), channel_id=1, replica_groups=mesh['rep'=4,'fsdp'=8] {'fsdp'}, use_global_device_ids=true, to_apply=%add | all-reduce | flops 128 | bytes 512
  42.8 16.7 %all-gather.8.cloned.1.call-done = bf16[1024,2048]{1,0:T(8,128)(2,1)} async-done(((bf16[128,2048]{1,0:T(8,128)(2,1)}), bf16[1024,2048]{1,0:T(8,128)(2,1)}) %all-gather.8.cloned.1.call-update) | async-done | bytes 4194320 | tf_op jit(solution)/shard_map/all_gather | solution.py:140
  59.5 3.1 fusion.40
  68.1 10.1 %all-gather.1 = bf16[8,1,128]{2,1,0:T(2,128)(2,1)S(1)} all-gather(bf16[1,1,128]{2,1,0:T(2,128)(2,1)S(1)} %bitcast.158), channel_id=1, replica_groups=mesh['rep'=4,'fsdp'=8] {'fsdp'}, dimensions={0}, use_global_device_ids=true | all-gather | bytes 2304 | tf_op jit(solution)/shard_map/all_gather | solution.py:147
  79.7 13.1 %all-gather.10.cloned.1.call-done = bf16[2,1024,512]{2,1,0:T(8,128)(2,1)} async-done(((bf16[2,128,512]{2,1,0:T(8,128)(2,1)}), bf16[2,1024,512]{2,1,0:T(8,128)(2,1)}) %all-gather.10.cloned.1.call-update) | async-done | bytes 2097168 | tf_op jit(solution)/shard_map/all_gather | solution.py:179
  92.8 2.6 fusion.42
  105.7 17.3 %all-gather.12.cloned.1.call-done = bf16[1024,1024]{1,0:T(8,128)(2,1)} async-done(((bf16[128,1024]{1,0:T(8,128)(2,1)}), bf16[1024,1024]{1,0:T(8,128)(2,1)}) %all-gather.12.cloned.1.call-update) | async-done | bytes 2097168 | tf_op jit(solution)/shard_map/all_gather | solution.py:141
  126.3 165.9 %all-gather.14.cloned.1.call-done = bf16[1024,9216]{1,0:T(8,128)(2,1)} async-done(((bf16[128,9216]{1,0:T(8,128)(2,1)}), bf16[1024,9216]{1,0:T(8,128)(2,1)}) %all-gather.14.cloned.1.call-update) | async-done | bytes 18874384 | tf_op jit(solution)/shard_map/all_gather | solution.py:142
  292.2 11.3 %fusion.41 = f32[128,9216]{1,0:T(8,128)} fusion(bf16[1024,9216]{1,0:T(8,128)(2,1)} %all-gather.14.cloned.1.call-done, f32[128,1024]{1,0:T(8,128)S(1)} %get-tuple-element.62, f32[1024]{0:T(1024)S(1)} %bitcast.143, f32[128]{0:T(128)S(1)} %get-tuple-element.58), kind=kOutput, calls=%fused_computation.114 | convolution fusion | flops 2416312320 | bytes 24121856 | tf_op jit(solution)/shard_map/dot_general | solution.py:189
  303.5 79.1 %all-gather.16.cloned.1.call-done = bf16[4608,1024]{1,0:T(8,128)(2,1)} async-done(((bf16[576,1024]{1,0:T(8,128)(2,1)}), bf16[4608,1024]{1,0:T(8,128)(2,1)}) %all-gather.16.cloned.1.call-update) | async-done | bytes 9437200 | tf_op jit(solution)/shard_map/all_gather | solution.py:143
  382.6 8.9 multiply_convert_fusion.1
  391.6 12.6 %multiply_reduce_fusion = (bf16[1024]{0:T(1024)(128)(2,1)}, f32[128]{0:T(128)S(1)}, f32[128,1024]{1,0:T(8,128)S(1)}) fusion(f32[128,1024]{1,0:T(8,128)S(1)} %get-tuple-element.62, f32[128]{0:T(128)S(1)} %copy-done.47, f32[1024]{0:T(1024)S(1)} %bitcast.144, bf16[1024,9216]{1,0:T(8,128)(2,1)} %all-gather.14.cloned.1.call-done, ...), kind=kOutput, calls=%fused_computation.39 | convolution fusion | flops 2421423104 | bytes 22289408 | tf_op jit(solution)/shard_map/dot_general | solution.py:121
  409.7 6.5 bitcast_convert_fusion
  416.3 5.7 fusion.2
  431.0 3.1 pad_maximum_fusion.1
  434.1 3.1 convolution_convert_fusion.3
  455.5 3.1 fusion.44
  478.4 4.4 convolution_convert_fusion.2
  483.8 5.1 convolution_convert_fusion.1
  489.6 10.9 %convolution_convert_fusion = bf16[1024,9216]{1,0:T(8,128)(2,1)} fusion(bf16[128,4608]{1,0:T(8,128)(2,1)} %copy-done.27, bf16[128,4608]{1,0:T(8,128)(2,1)} %copy-done.26, f32[128,1024]{1,0:T(8,128)S(1)} %get-tuple-element.62, f32[1024]{0:T(1024)S(1)} %bitcast.146, f32[128]{0:T(128)S(1)} %copy-done.48), kind=kOutput, calls=%fused_computation | convolution fusion | flops 2430468096 | bytes 21762560 | tf_op jit(solution)/shard_map/dot_general | solution.py:115
  500.8 4.7 reduce-scatter.10.cloned.1.call-done
  505.5 51.2 %reduce-scatter.8.cloned.1.call-done = bf16[128,2048]{1,0:T(8,128)(2,1)} async-done(((bf16[1024,2048]{1,0:T(8,128)(2,1)}), bf16[128,2048]{1,0:T(8,128)(2,1)}) %reduce-scatter.8.cloned.1.call-update) | async-done | bytes 524304 | tf_op jit(solution)/shard_map/reduce_scatter | solution.py:277
  556.7 100.2 %reduce-scatter.14.cloned.1.call-done = bf16[576,1024]{1,0:T(8,128)(2,1)} async-done(((bf16[4608,1024]{1,0:T(8,128)(2,1)}), bf16[576,1024]{1,0:T(8,128)(2,1)}) %reduce-scatter.14.cloned.1.call-update) | async-done | bytes 1179664 | tf_op jit(solution)/shard_map/reduce_scatter | solution.py:286
  657.0 188.6 %reduce-scatter.12.cloned.1.call-done = bf16[128,9216]{1,0:T(8,128)(2,1)} async-done(((bf16[1024,9216]{1,0:T(8,128)(2,1)}), bf16[128,9216]{1,0:T(8,128)(2,1)}) %reduce-scatter.12.cloned.1.call-update) | async-done | bytes 2359312 | tf_op jit(solution)/shard_map/reduce_scatter | solution.py:283
  852.3 3.3 fusion.15
  855.5 5.9 convolution_add_fusion.1
  863.5 4.0 multiply_reduce_fusion.1
  867.5 14.3 %all-reduce.6 = (bf16[1024]{0:T(1024)(128)(2,1)S(1)}, bf16[64]{0:T(256)(128)(2,1)S(1)}, bf16[64]{0:T(256)(128)(2,1)S(1)}, bf16[1024]{0:T(1024)(128)(2,1)S(1)}) all-reduce(bf16[1024]{0:T(1024)(128)(2,1)S(1)} %get-tuple-element.12, bf16[64]{0:T(256)(128)(2,1)S(1)} %copy-done.56, ...), channel_id=7, replica_groups=mesh['rep'=4,'fsdp'=8] {'fsdp'}, use_global_device_ids=true, to_apply=%region_21.22.clone | all-reduce | flops 2176 | bytes 8704
  882.0 10.3 %all-reduce.8 = (bf16[128]{0:T(256)(128)(2,1)S(1)}, bf16[8]{0:T(256)(128)(2,1)S(1)}, bf16[8]{0:T(256)(128)(2,1)S(1)}, bf16[128]{0:T(256)(128)(2,1)S(1)}) all-reduce(bf16[128]{0:T(256)(128)(2,1)S(1)} %dynamic-slice.3, bf16[8]{0:T(256)(128)(2,1)S(1)} %dynamic-slice.5, ...), channel_id=1, replica_groups=mesh['rep'=4,'fsdp'=8] {'rep'}, use_global_device_ids=true, to_apply=%region_22.23 | all-reduce | flops 272 | bytes 1088 | tf_op jit(solution)/shard_map/psum | solution.py:307
  895.4 58.3 %all-reduce.12.cloned.1.call-done = (bf16[128,2048]{1,0:T(8,128)(2,1)}, bf16[128,1024]{1,0:T(8,128)(2,1)}, bf16[128,9216]{1,0:T(8,128)(2,1)}, bf16[576,1024]{1,0:T(8,128)(2,1)}) async-done(((bf16[128,2048]{1,0:T(8,128)(2,1)}, bf16[128,1024]{1,0:T(8,128)(2,1)}, bf16[128,9216]{1,0:T(8,128)(2,1)}, bf16[576,1024]{1,0:T(8,128)(2,1)}), (bf16[128,2048]{1,0:T(8,128)(2,1)}, bf16[128,1024]{1,0:T(8,128)(2,1)}, ...) | async-done | bytes 4325392 | tf_op jit(solution)/shard_map/psum | solution.py:303
  953.7 4.4 convert_element_type.164
  (249 shorter events, 95.0 us)
Async XLA Ops:
  7.2 52.3 %all-gather.8.cloned.1.call-start = ((), (), s32[]{:S(2)}) async-start(), calls=%async_computation.5 | async-start | bytes 4718592 | tf_op jit(solution)/shard_map/all_gather | solution.py:140
  7.9 84.9 %all-gather.10.cloned.1.call-start = ((), (), s32[]{:S(2)}) async-start(), calls=%async_computation.6 | async-start | bytes 2359296 | tf_op jit(solution)/shard_map/all_gather | solution.py:179
  40.3 26.4 %copy-start.61 = (bf16[64]{0:T(256)(128)(2,1)}, bf16[64]{0:T(256)(128)(2,1)S(1)}, u32[]{:S(2)}) copy-start(bf16[64]{0:T(256)(128)(2,1)S(1)} %get-tuple-element.19) | copy-start | bytes 388
  40.3 23.4 %copy-start.55 = (f32[64]{0:T(128)}, f32[64]{0:T(128)S(1)}, u32[]{:S(2)}) copy-start(f32[64]{0:T(128)S(1)} %convert_element_type.142) | copy-start | bytes 772
  42.6 20.1 %copy-start.50 = (f32[128]{0:T(128)}, f32[128]{0:T(128)S(1)}, u32[]{:S(2)}) copy-start(f32[128]{0:T(128)S(1)} %get-tuple-element.56) | copy-start | bytes 1540
  42.8 36.8 %copy-start.39 = (f32[128,32]{0,1:T(8,128)}, f32[128,32]{0,1:T(8,128)S(1)}, u32[]{:S(2)}) copy-start(f32[128,32]{0,1:T(8,128)S(1)} %get-tuple-element.51) | copy-start | bytes 49156
  42.8 36.8 %copy-start.41 = (f32[128,32]{0,1:T(8,128)}, f32[128,32]{0,1:T(8,128)S(1)}, u32[]{:S(2)}) copy-start(f32[128,32]{0,1:T(8,128)S(1)} %get-tuple-element.52) | copy-start | bytes 49156
  62.6 15.8 %copy-start.8 = (f32[128,2048]{1,0:T(8,128)}, f32[128,2048]{1,0:T(8,128)S(1)}, u32[]{:S(2)}) copy-start(f32[128,2048]{1,0:T(8,128)S(1)} %fusion.40) | copy-start | bytes 3145732
  64.7 58.3 %all-gather.12.cloned.1.call-start = ((), (), s32[]{:S(2)}) async-start(), calls=%async_computation.7 | async-start | bytes 2359296 | tf_op jit(solution)/shard_map/all_gather | solution.py:141
  65.4 226.8 %all-gather.14.cloned.1.call-start = ((), (), s32[]{:S(2)}) async-start(), calls=%async_computation.8 | async-start | bytes 21233664 | tf_op jit(solution)/shard_map/all_gather | solution.py:142
  66.0 316.6 %all-gather.16.cloned.1.call-start = ((), (), s32[]{:S(2)}) async-start(), calls=%async_computation.9 | async-start | bytes 10616832 | tf_op jit(solution)/shard_map/all_gather | solution.py:143
  66.6 402.0 %reduce-scatter.6.cloned.1.call-start = ((), (), s32[]{:S(2)}) async-start(), calls=%async_computation.10 | async-start | bytes 2359296 | tf_op jit(solution)/shard_map/reduce_scatter | solution.py:229
  66.7 28.8 %copy-start.52 = (f32[64]{0:T(128)}, f32[64]{0:T(128)S(1)}, u32[]{:S(2)}) copy-start(f32[64]{0:T(128)S(1)} %convert_element_type.145) | copy-start | bytes 772
  78.4 23.3 %copy-start.20 = (pred[128,1024]{0,1:T(8,128)(4,1)}, pred[128,1024]{0,1:T(8,128)(4,1)S(1)}, u32[]{:S(2)}) copy-start(pred[128,1024]{0,1:T(8,128)(4,1)S(1)} %fusion.18) | copy-start | bytes 393220
  78.5 17.0 %copy-start.10 = (f32[128,1024]{1,0:T(8,128)}, f32[128,1024]{1,0:T(8,128)S(1)}, u32[]{:S(2)}) copy-start(f32[128,1024]{1,0:T(8,128)S(1)} %slice.77) | copy-start | bytes 1572868
  78.7 18.3 %copy-start.4 = (f32[128,1024]{0,1:T(8,128)}, f32[128,1024]{0,1:T(8,128)S(1)}, u32[]{:S(2)}) copy-start(f32[128,1024]{0,1:T(8,128)S(1)} %copy.98) | copy-start | bytes 1572868
  79.7 18.6 %copy-start.22 = (bf16[128,16,32]{0,2,1:T(8,128)(2,1)}, bf16[128,16,32]{0,2,1:T(8,128)(2,1)S(1)}, u32[]{:S(2)}) copy-start(bf16[128,16,32]{0,2,1:T(8,128)(2,1)S(1)} %get-tuple-element.35) | copy-start | bytes 393220
  79.7 18.6 %copy-start.24 = (bf16[128,16,32]{0,2,1:T(8,128)(2,1)}, bf16[128,16,32]{0,2,1:T(8,128)(2,1)S(1)}, u32[]{:S(2)}) copy-start(bf16[128,16,32]{0,2,1:T(8,128)(2,1)S(1)} %get-tuple-element.36) | copy-start | bytes 393220
  103.1 19.9 %copy-start.2 = (f32[128,1024]{1,0:T(8,128)S(1)}, f32[128,1024]{1,0:T(8,128)}, u32[]{:S(2)}) copy-start(f32[128,1024]{1,0:T(8,128)} %param.11) | copy-start | bytes 1572868
  105.7 197.9 %copy-start.17 = (bf16[8,64,2,128]{3,1,2,0:T(8,128)(2,1)}, bf16[8,64,2,128]{3,1,2,0:T(8,128)(2,1)S(1)}, u32[]{:S(2)}) copy-start(bf16[8,64,2,128]{3,1,2,0:T(8,128)(2,1)S(1)} %fusion.13) | copy-start | bytes 786436
  125.7 177.8 %copy-start.46 = (f32[128]{0:T(128)}, f32[128]{0:T(128)S(1)}, u32[]{:S(2)}) copy-start(f32[128]{0:T(128)S(1)} %get-tuple-element.58) | copy-start | bytes 1540
  434.0 71.5 %reduce-scatter.10.cloned.1.call-start = ((), (), s32[]{:S(2)}) async-start(), calls=%async_computation.12 | async-start | bytes 2359296 | tf_op jit(solution)/shard_map/reduce_scatter | solution.py:280
  437.2 119.5 %reduce-scatter.8.cloned.1.call-start = ((), (), s32[]{:S(2)}) async-start(), calls=%async_computation.11 | async-start | bytes 4718592 | tf_op jit(solution)/shard_map/reduce_scatter | solution.py:277
  482.8 174.2 %reduce-scatter.14.cloned.1.call-start = ((), (), s32[]{:S(2)}) async-start(), calls=%async_computation.14 | async-start | bytes 10616832 | tf_op jit(solution)/shard_map/reduce_scatter | solution.py:286
  488.9 356.6 %reduce-scatter.12.cloned.1.call-start = ((), (), s32[]{:S(2)}) async-start(), calls=%async_computation.13 | async-start | bytes 21233664 | tf_op jit(solution)/shard_map/reduce_scatter | solution.py:283
  500.5 346.5 %copy-start.11 = (f32[128,1024]{1,0:T(8,128)S(1)}, f32[128,1024]{1,0:T(8,128)}, u32[]{:S(2)}) copy-start(f32[128,1024]{1,0:T(8,128)} %copy-done.10) | copy-start | bytes 1572868
  500.5 347.7 %copy-start.45 = (f32[128,8]{0,1:T(8,128)S(1)}, f32[128,8]{0,1:T(8,128)}, u32[]{:S(2)}) copy-start(f32[128,8]{0,1:T(8,128)} %copy-done.44) | copy-start | bytes 12292
  500.5 347.8 %copy-start.13 = (f32[128,512]{1,0:T(8,128)S(1)}, f32[128,512]{1,0:T(8,128)}, u32[]{:S(2)}) copy-start(f32[128,512]{1,0:T(8,128)} %copy-done.12) | copy-start | bytes 786436
  500.5 350.4 %copy-start.15 = (f32[128,16,32]{0,2,1:T(8,128)S(1)}, f32[128,16,32]{0,2,1:T(8,128)}, u32[]{:S(2)}) copy-start(f32[128,16,32]{0,2,1:T(8,128)} %copy-done.14) | copy-start | bytes 786436
  500.6 453.1 %all-reduce.12.cloned.1.call-start = ((), (), s32[]{:S(2)}) async-start(), calls=%async_computation.15 | async-start | bytes 8650752 | tf_op jit(solution)/shard_map/psum | solution.py:303
  861.7 32.7 %copy-start.7 = (f32[128,1024]{1,0:T(8,128)S(1)}, f32[128,1024]{1,0:T(8,128)}, u32[]{:S(2)}) copy-start(f32[128,1024]{1,0:T(8,128)} %copy-done.6) | copy-start | bytes 1572868
  861.7 32.7 %copy-start.57 = (f32[128]{0:T(128)S(1)}, f32[128]{0:T(128)}, u32[]{:S(2)}) copy-start(f32[128]{0:T(128)} %get-tuple-element.55) | copy-start | bytes 1540
  (41 other events, 229.0 us)
Sparse Core Ops, SparseCore 0:
  9.6 49.8 all-gather.7
  64.8 27.9 all-gather.9
  94.4 28.5 all-gather.11
  124.5 167.6 all-gather.13
  293.7 88.8 all-gather.15
  434.1 34.4 reduce-scatter.5
  470.9 34.5 reduce-scatter.9
  508.4 48.2 reduce-scatter.7
  559.0 97.8 reduce-scatter.13
  659.2 186.3 reduce-scatter.11
  849.3 104.2 all-reduce.11
where the time goes:
time: 972 us; the launch traced here: 968 us
  waiting for transfers between devices  699 us (72%)
  matrix products  94.7 us (10%)
  blocking collectives  63.3 us (7%)
  local copies, waits for them, and re-layouts  56.8 us (6%)
  other arithmetic  36.6 us (4%)
  between operations  16.9 us (2%)
    reduce_scatter x1, waiting for transfers between devices, body(): lax.psum_scatter(grads_local[2].astype(jnp.bfloat16), 'fsdp', scatter_dim...  189 us
    all_gather x1, waiting for transfers between devices, body(): lax.all_gather(shards[2], 'fsdp', axis=0, tiled=True)  166 us
    reduce_scatter x1, waiting for transfers between devices, body(): lax.psum_scatter(grads_local[3].astype(jnp.bfloat16), 'fsdp', scatter_dim...  100 us
    all_gather x1, waiting for transfers between devices, body(): lax.all_gather(shards[3], 'fsdp', axis=0, tiled=True)  79.1 us
    psum x1, waiting for transfers between devices, body(): lax.psum(grad_share[0].astype(jnp.bfloat16), 'rep').astype(jnp.float32)  58.3 us
    reduce_scatter x1, waiting for transfers between devices, body(): lax.psum_scatter(grads_local[0].astype(jnp.bfloat16), 'fsdp', scatter_dim...  51.2 us
    unnamed x2, blocking collectives  29.3 us
    dot_general x4, matrix products, transposed_product(): lax.dot_general(left_arr, right_arr, (((1,), (1,)), ((), ())), preferred_...  27 us
  transfers between devices with their start and end apart: 11, of which 11 were waited for; matrix products, arithmetic and copies ran while one was open for 12% of the time, Pallas kernels for 0%

commit v1 on v0

--- a/solution.py
+++ b/solution.py
@@ -300,7 +300,9 @@
         ).astype(jnp.float32),
     )
     grad_total = (
-        lax.psum(grad_share[0].astype(jnp.bfloat16), "rep").astype(jnp.float32),
+        jnp.sum(lax.all_gather(grad_share[0].astype(jnp.bfloat16), "rep"), axis=0).astype(
+            jnp.float32
+        ),
         lax.psum(grad_share[1].astype(jnp.bfloat16), "rep").astype(jnp.float32),
         lax.psum(grad_share[2].astype(jnp.bfloat16), "rep").astype(jnp.float32),
         lax.psum(grad_share[3].astype(jnp.bfloat16), "rep").astype(jnp.float32),

time: 972 us -> 1010 us (1.039)
  waiting for transfers between devices: 699 us -> 735 us
    reduce_scatter x1, waiting for transfers between devices: 4.73 us -> 37 us  [body(): lax.psum_scatter(grads_local[1].astype(jnp.bfloat16), 'fsdp', scatter_dim...]
    reduce_scatter x1, waiting for transfers between devices: 51.2 us -> 27.7 us  [body(): lax.psum_scatter(grads_local[0].astype(jnp.bfloat16), 'fsdp', scatter_dim...]
    psum x1, waiting for transfers between devices: 58.3 us -> 81.8 us  [body(): lax.psum(grad_share[1].astype(jnp.bfloat16), 'rep').astype(jnp.float32)]
  transfers between devices with their start and end apart: 11 -> 12, of which waited for: 11 -> 11; matrix products, arithmetic and copies ran while one was open for 12% -> 11% of each run, Pallas kernels for 0% -> 0%
where the time goes in v1:
time: 1010 us
  waiting for transfers between devices  735 us (73%)
  matrix products  95.2 us (9%)
  blocking collectives  62.6 us (6%)
  local copies, waits for them, and re-layouts  60 us (6%)
  other arithmetic  38 us (4%)
  between operations  17.2 us (2%)
    reduce_scatter x1, waiting for transfers between devices, body(): lax.psum_scatter(grads_local[2].astype(jnp.bfloat16), 'fsdp', scatter_dim...  189 us
    all_gather x1, waiting for transfers between devices, body(): lax.all_gather(shards[2], 'fsdp', axis=0, tiled=True)  166 us
    reduce_scatter x1, waiting for transfers between devices, body(): lax.psum_scatter(grads_local[3].astype(jnp.bfloat16), 'fsdp', scatter_dim...  100 us
    psum x1, waiting for transfers between devices, body(): lax.psum(grad_share[1].astype(jnp.bfloat16), 'rep').astype(jnp.float32)  81.8 us
    all_gather x1, waiting for transfers between devices, body(): lax.all_gather(shards[3], 'fsdp', axis=0, tiled=True)  79.1 us
    reduce_scatter x1, waiting for transfers between devices, body(): lax.psum_scatter(grads_local[1].astype(jnp.bfloat16), 'fsdp', scatter_dim...  37 us
    unnamed x2, blocking collectives  28.9 us
    reduce_scatter x1, waiting for transfers between devices, body(): lax.psum_scatter(grads_local[0].astype(jnp.bfloat16), 'fsdp', scatter_dim...  27.7 us
  transfers between devices with their start and end apart: 12, of which 11 were waited for; matrix products, arithmetic and copies ran while one was open for 11% of the time, Pallas kernels for 0%

profile of v1, /device:TPU:0, one launch (start us, length us, event | category | flops | bytes accessed | tf_op | source)
XLA Modules:
  0.0 1008.9 jit_solution(15651389630529209557)
XLA Ops:
  8.0 13.6 %all-gather.1 = bf16[8,1,128]{2,1,0:T(2,128)(2,1)S(1)} all-gather(bf16[1,1,128]{2,1,0:T(2,128)(2,1)} %bitcast.159), channel_id=1, replica_groups=mesh['rep'=4,'fsdp'=8] {'fsdp'}, dimensions={0}, use_global_device_ids=true | all-gather | bytes 2304 | tf_op jit(solution)/shard_map/all_gather | solution.py:144
  25.3 15.0 %all-reduce.7 = (bf16[64]{0:T(256)(128)(2,1)S(1)}, bf16[64]{0:T(256)(128)(2,1)S(1)}) all-reduce(bf16[64]{0:T(256)(128)(2,1)S(1)} %dynamic-update-slice, bf16[64]{0:T(256)(128)(2,1)S(1)} %dynamic-update-slice.1), channel_id=1, replica_groups=mesh['rep'=4,'fsdp'=8] {'fsdp'}, use_global_device_ids=true, to_apply=%add | all-reduce | flops 128 | bytes 512
  42.8 16.7 %all-gather.10.cloned.1.call-done = bf16[1024,2048]{1,0:T(8,128)(2,1)} async-done(((bf16[128,2048]{1,0:T(8,128)(2,1)}), bf16[1024,2048]{1,0:T(8,128)(2,1)}) %all-gather.10.cloned.1.call-update) | async-done | bytes 4194320 | tf_op jit(solution)/shard_map/all_gather | solution.py:140
  59.5 3.1 fusion.40
  68.2 10.1 all-gather.2
  79.8 13.1 %all-gather.12.cloned.1.call-done = bf16[2,1024,512]{2,1,0:T(8,128)(2,1)} async-done(((bf16[2,128,512]{2,1,0:T(8,128)(2,1)}), bf16[2,1024,512]{2,1,0:T(8,128)(2,1)}) %all-gather.12.cloned.1.call-update) | async-done | bytes 2097168 | tf_op jit(solution)/shard_map/all_gather | solution.py:179
  92.8 2.6 fusion.42
  103.1 2.5 fusion.13
  105.7 17.3 %all-gather.14.cloned.1.call-done = bf16[1024,1024]{1,0:T(8,128)(2,1)} async-done(((bf16[128,1024]{1,0:T(8,128)(2,1)}), bf16[1024,1024]{1,0:T(8,128)(2,1)}) %all-gather.14.cloned.1.call-update) | async-done | bytes 2097168 | tf_op jit(solution)/shard_map/all_gather | solution.py:141
  126.3 165.9 %all-gather.16.cloned.1.call-done = bf16[1024,9216]{1,0:T(8,128)(2,1)} async-done(((bf16[128,9216]{1,0:T(8,128)(2,1)}), bf16[1024,9216]{1,0:T(8,128)(2,1)}) %all-gather.16.cloned.1.call-update) | async-done | bytes 18874384 | tf_op jit(solution)/shard_map/all_gather | solution.py:142
  292.2 11.3 %fusion.41 = f32[128,9216]{1,0:T(8,128)} fusion(bf16[1024,9216]{1,0:T(8,128)(2,1)} %all-gather.16.cloned.1.call-done, f32[128,1024]{1,0:T(8,128)S(1)} %get-tuple-element.61, f32[1024]{0:T(1024)S(1)} %bitcast.145, f32[128]{0:T(128)S(1)} %get-tuple-element.57), kind=kOutput, calls=%fused_computation.114 | convolution fusion | flops 2416312320 | bytes 24121856 | tf_op jit(solution)/shard_map/dot_general | solution.py:189
  303.5 79.1 %all-gather.18.cloned.1.call-done = bf16[4608,1024]{1,0:T(8,128)(2,1)} async-done(((bf16[576,1024]{1,0:T(8,128)(2,1)}), bf16[4608,1024]{1,0:T(8,128)(2,1)}) %all-gather.18.cloned.1.call-update) | async-done | bytes 9437200 | tf_op jit(solution)/shard_map/all_gather | solution.py:143
  382.6 8.9 multiply_convert_fusion.1
  391.6 12.6 %multiply_reduce_fusion = (bf16[1024]{0:T(1024)(128)(2,1)}, f32[128]{0:T(128)S(1)}, f32[128,1024]{1,0:T(8,128)S(1)}) fusion(f32[128,1024]{1,0:T(8,128)S(1)} %get-tuple-element.61, f32[128]{0:T(128)S(1)} %copy-done.44, f32[1024]{0:T(1024)S(1)} %bitcast.146, bf16[1024,9216]{1,0:T(8,128)(2,1)} %all-gather.16.cloned.1.call-done, ...), kind=kOutput, calls=%fused_computation.39 | convolution fusion | flops 2421423104 | bytes 22289408 | tf_op jit(solution)/shard_map/dot_general | solution.py:121
  409.8 6.5 bitcast_convert_fusion
  416.3 5.7 fusion.2
  431.0 3.1 pad_maximum_fusion.1
  452.3 3.1 fusion.44
  463.9 4.8 reduce-scatter.6.cloned.1.call-done
  478.5 4.4 convolution_convert_fusion.2
  486.1 6.1 convolution_convert_fusion.1
  492.9 11.0 %convolution_convert_fusion = bf16[1024,9216]{1,0:T(8,128)(2,1)} fusion(bf16[128,4608]{1,0:T(8,128)(2,1)} %copy-done.26, bf16[128,4608]{1,0:T(8,128)(2,1)} %copy-done.25, f32[128,1024]{1,0:T(8,128)S(1)} %get-tuple-element.61, f32[1024]{0:T(1024)S(1)} %bitcast.148, f32[128]{0:T(128)S(1)} %copy-done.45), kind=kOutput, calls=%fused_computation | convolution fusion | flops 2430468096 | bytes 21762560 | tf_op jit(solution)/shard_map/dot_general | solution.py:115
  503.9 27.7 %reduce-scatter.8.cloned.1.call-done = bf16[128,2048]{1,0:T(8,128)(2,1)} async-done(((bf16[1024,2048]{1,0:T(8,128)(2,1)}), bf16[128,2048]{1,0:T(8,128)(2,1)}) %reduce-scatter.8.cloned.1.call-update) | async-done | bytes 524304 | tf_op jit(solution)/shard_map/reduce_scatter | solution.py:277
  531.9 37.0 %reduce-scatter.10.cloned.1.call-done = bf16[128,1024]{1,0:T(8,128)(2,1)} async-done(((bf16[1024,1024]{1,0:T(8,128)(2,1)}), bf16[128,1024]{1,0:T(8,128)(2,1)}) %reduce-scatter.10.cloned.1.call-update) | async-done | bytes 262160 | tf_op jit(solution)/shard_map/reduce_scatter | solution.py:280
  568.9 100.5 %reduce-scatter.14.cloned.1.call-done = bf16[576,1024]{1,0:T(8,128)(2,1)} async-done(((bf16[4608,1024]{1,0:T(8,128)(2,1)}), bf16[576,1024]{1,0:T(8,128)(2,1)}) %reduce-scatter.14.cloned.1.call-update) | async-done | bytes 1179664 | tf_op jit(solution)/shard_map/reduce_scatter | solution.py:286
  669.3 188.6 %reduce-scatter.12.cloned.1.call-done = bf16[128,9216]{1,0:T(8,128)(2,1)} async-done(((bf16[1024,9216]{1,0:T(8,128)(2,1)}), bf16[128,9216]{1,0:T(8,128)(2,1)}) %reduce-scatter.12.cloned.1.call-update) | async-done | bytes 2359312 | tf_op jit(solution)/shard_map/reduce_scatter | solution.py:283
  870.4 5.9 convolution_add_fusion.1
  878.2 4.4 multiply_reduce_fusion.1
  882.7 13.9 %all-reduce.6 = (bf16[1024]{0:T(1024)(128)(2,1)S(1)}, bf16[64]{0:T(256)(128)(2,1)S(1)}, bf16[64]{0:T(256)(128)(2,1)S(1)}, bf16[1024]{0:T(1024)(128)(2,1)S(1)}) all-reduce(bf16[1024]{0:T(1024)(128)(2,1)S(1)} %get-tuple-element.12, bf16[64]{0:T(256)(128)(2,1)S(1)} %fusion.15, ...), channel_id=8, replica_groups=mesh['rep'=4,'fsdp'=8] {'fsdp'}, use_global_device_ids=true, to_apply=%region_21.22.clone | all-reduce | flops 2176 | bytes 8704
  896.9 10.0 all-reduce.8
  913.0 81.8 %all-reduce.12.cloned.1.call-done = (bf16[128,1024]{1,0:T(8,128)(2,1)}, bf16[128,9216]{1,0:T(8,128)(2,1)}, bf16[576,1024]{1,0:T(8,128)(2,1)}) async-done(((bf16[128,1024]{1,0:T(8,128)(2,1)}, bf16[128,9216]{1,0:T(8,128)(2,1)}, bf16[576,1024]{1,0:T(8,128)(2,1)}), (bf16[128,1024]{1,0:T(8,128)(2,1)}, bf16[128,9216]{1,0:T(8,128)(2,1)}, bf16[576,1024]{1,0:T(8,128)(2,1)})) %all-reduce.12.cloned.1.call-update) | async-done | bytes 3801104 | tf_op jit(solution)/shard_map/psum | solution.py:306
  994.8 4.4 convert_element_type.166
  (245 shorter events, 100.8 us)
Async XLA Ops:
  7.2 52.3 %all-gather.10.cloned.1.call-start = ((), (), s32[]{:S(2)}) async-start(), calls=%async_computation.5 | async-start | bytes 4718592 | tf_op jit(solution)/shard_map/all_gather | solution.py:140
  7.9 84.9 %all-gather.12.cloned.1.call-start = ((), (), s32[]{:S(2)}) async-start(), calls=%async_computation.6 | async-start | bytes 2359296 | tf_op jit(solution)/shard_map/all_gather | solution.py:179
  40.3 26.4 %copy-start.57 = (bf16[64]{0:T(256)(128)(2,1)}, bf16[64]{0:T(256)(128)(2,1)S(1)}, u32[]{:S(2)}) copy-start(bf16[64]{0:T(256)(128)(2,1)S(1)} %get-tuple-element.19) | copy-start | bytes 388
  40.3 23.4 %copy-start.52 = (f32[64]{0:T(128)}, f32[64]{0:T(128)S(1)}, u32[]{:S(2)}) copy-start(f32[64]{0:T(128)S(1)} %convert_element_type.144) | copy-start | bytes 772
  42.6 20.1 %copy-start.47 = (f32[128]{0:T(128)}, f32[128]{0:T(128)S(1)}, u32[]{:S(2)}) copy-start(f32[128]{0:T(128)S(1)} %get-tuple-element.55) | copy-start | bytes 1540
  42.8 36.9 %copy-start.36 = (f32[128,32]{0,1:T(8,128)}, f32[128,32]{0,1:T(8,128)S(1)}, u32[]{:S(2)}) copy-start(f32[128,32]{0,1:T(8,128)S(1)} %get-tuple-element.50) | copy-start | bytes 49156
  42.8 36.9 %copy-start.38 = (f32[128,32]{0,1:T(8,128)}, f32[128,32]{0,1:T(8,128)S(1)}, u32[]{:S(2)}) copy-start(f32[128,32]{0,1:T(8,128)S(1)} %get-tuple-element.51) | copy-start | bytes 49156
  62.6 15.8 %copy-start.8 = (f32[128,2048]{1,0:T(8,128)}, f32[128,2048]{1,0:T(8,128)S(1)}, u32[]{:S(2)}) copy-start(f32[128,2048]{1,0:T(8,128)S(1)} %fusion.40) | copy-start | bytes 3145732
  62.7 15.5 %copy-start.12 = (f32[128,512]{1,0:T(8,128)}, f32[128,512]{1,0:T(8,128)S(1)}, u32[]{:S(2)}) copy-start(f32[128,512]{1,0:T(8,128)S(1)} %slice.71) | copy-start | bytes 786436
  64.7 58.3 %all-gather.14.cloned.1.call-start = ((), (), s32[]{:S(2)}) async-start(), calls=%async_computation.7 | async-start | bytes 2359296 | tf_op jit(solution)/shard_map/all_gather | solution.py:141
  65.4 226.8 %all-gather.16.cloned.1.call-start = ((), (), s32[]{:S(2)}) async-start(), calls=%async_computation.8 | async-start | bytes 21233664 | tf_op jit(solution)/shard_map/all_gather | solution.py:142
  66.0 316.6 %all-gather.18.cloned.1.call-start = ((), (), s32[]{:S(2)}) async-start(), calls=%async_computation.9 | async-start | bytes 10616832 | tf_op jit(solution)/shard_map/all_gather | solution.py:143
  66.6 402.1 %reduce-scatter.6.cloned.1.call-start = ((), (), s32[]{:S(2)}) async-start(), calls=%async_computation.10 | async-start | bytes 2359296 | tf_op jit(solution)/shard_map/reduce_scatter | solution.py:229
  66.7 28.8 %copy-start.49 = (f32[64]{0:T(128)}, f32[64]{0:T(128)S(1)}, u32[]{:S(2)}) copy-start(f32[64]{0:T(128)S(1)} %convert_element_type.147) | copy-start | bytes 772
  78.5 23.3 %copy-start.19 = (pred[128,1024]{0,1:T(8,128)(4,1)}, pred[128,1024]{0,1:T(8,128)(4,1)S(1)}, u32[]{:S(2)}) copy-start(pred[128,1024]{0,1:T(8,128)(4,1)S(1)} %fusion.18) | copy-start | bytes 393220
  78.5 17.0 %copy-start.10 = (f32[128,1024]{1,0:T(8,128)}, f32[128,1024]{1,0:T(8,128)S(1)}, u32[]{:S(2)}) copy-start(f32[128,1024]{1,0:T(8,128)S(1)} %slice.77) | copy-start | bytes 1572868
  78.7 18.3 %copy-start.4 = (f32[128,1024]{0,1:T(8,128)}, f32[128,1024]{0,1:T(8,128)S(1)}, u32[]{:S(2)}) copy-start(f32[128,1024]{0,1:T(8,128)S(1)} %copy.98) | copy-start | bytes 1572868
  79.7 18.6 %copy-start.21 = (bf16[128,16,32]{0,2,1:T(8,128)(2,1)}, bf16[128,16,32]{0,2,1:T(8,128)(2,1)S(1)}, u32[]{:S(2)}) copy-start(bf16[128,16,32]{0,2,1:T(8,128)(2,1)S(1)} %get-tuple-element.34) | copy-start | bytes 393220
  79.7 18.6 %copy-start.23 = (bf16[128,16,32]{0,2,1:T(8,128)(2,1)}, bf16[128,16,32]{0,2,1:T(8,128)(2,1)S(1)}, u32[]{:S(2)}) copy-start(bf16[128,16,32]{0,2,1:T(8,128)(2,1)S(1)} %get-tuple-element.35) | copy-start | bytes 393220
  103.1 19.9 %copy-start.2 = (f32[128,1024]{1,0:T(8,128)S(1)}, f32[128,1024]{1,0:T(8,128)}, u32[]{:S(2)}) copy-start(f32[128,1024]{1,0:T(8,128)} %param.11) | copy-start | bytes 1572868
  105.7 197.9 %copy-start.16 = (bf16[8,64,2,128]{3,1,2,0:T(8,128)(2,1)}, bf16[8,64,2,128]{3,1,2,0:T(8,128)(2,1)S(1)}, u32[]{:S(2)}) copy-start(bf16[8,64,2,128]{3,1,2,0:T(8,128)(2,1)S(1)} %fusion.13) | copy-start | bytes 786436
  125.7 177.8 %copy-start.43 = (f32[128]{0:T(128)}, f32[128]{0:T(128)S(1)}, u32[]{:S(2)}) copy-start(f32[128]{0:T(128)S(1)} %get-tuple-element.57) | copy-start | bytes 1540
  434.1 97.5 %reduce-scatter.8.cloned.1.call-start = ((), (), s32[]{:S(2)}) async-start(), calls=%async_computation.11 | async-start | bytes 4718592 | tf_op jit(solution)/shard_map/reduce_scatter | solution.py:277
  482.9 86.0 %reduce-scatter.10.cloned.1.call-start = ((), (), s32[]{:S(2)}) async-start(), calls=%async_computation.12 | async-start | bytes 2359296 | tf_op jit(solution)/shard_map/reduce_scatter | solution.py:280
  486.0 183.3 %reduce-scatter.14.cloned.1.call-start = ((), (), s32[]{:S(2)}) async-start(), calls=%async_computation.14 | async-start | bytes 10616832 | tf_op jit(solution)/shard_map/reduce_scatter | solution.py:286
  492.2 365.7 %reduce-scatter.12.cloned.1.call-start = ((), (), s32[]{:S(2)}) async-start(), calls=%async_computation.13 | async-start | bytes 21233664 | tf_op jit(solution)/shard_map/reduce_scatter | solution.py:283
  503.9 356.1 %copy-start.11 = (f32[128,1024]{1,0:T(8,128)S(1)}, f32[128,1024]{1,0:T(8,128)}, u32[]{:S(2)}) copy-start(f32[128,1024]{1,0:T(8,128)} %copy-done.10) | copy-start | bytes 1572868
  503.9 357.4 %copy-start.42 = (f32[128,8]{0,1:T(8,128)S(1)}, f32[128,8]{0,1:T(8,128)}, u32[]{:S(2)}) copy-start(f32[128,8]{0,1:T(8,128)} %copy-done.41) | copy-start | bytes 12292
  503.9 357.4 %copy-start.13 = (f32[128,512]{1,0:T(8,128)S(1)}, f32[128,512]{1,0:T(8,128)}, u32[]{:S(2)}) copy-start(f32[128,512]{1,0:T(8,128)} %copy-done.12) | copy-start | bytes 786436
  503.9 406.0 %all-gather.20.cloned.1.call-start = ((), (), s32[]{:S(2)}) async-start(), calls=%async_computation.15 | async-start | bytes 2621440 | tf_op jit(solution)/shard_map/all_gather | solution.py:303
  531.6 463.2 %all-reduce.12.cloned.1.call-start = ((), (), s32[]{:S(2)}) async-start(), calls=%async_computation.16 | async-start | bytes 7602176 | tf_op jit(solution)/shard_map/psum | solution.py:306
  876.6 32.4 %copy-start.53 = (f32[128]{0:T(128)S(1)}, f32[128]{0:T(128)}, u32[]{:S(2)}) copy-start(f32[128]{0:T(128)} %get-tuple-element.54) | copy-start | bytes 1540
  (38 other events, 198.6 us)
Sparse Core Ops, SparseCore 0:
  9.6 49.8 all-gather.9
  64.8 27.9 all-gather.11
  94.4 28.5 all-gather.13
  124.5 167.6 all-gather.15
  293.7 88.8 all-gather.17
  434.2 34.4 reduce-scatter.5
  483.0 48.5 reduce-scatter.7
  534.5 34.3 reduce-scatter.9
  571.2 98.1 reduce-scatter.13
  671.5 186.3 reduce-scatter.11
  859.8 33.6 all-gather.19
  896.7 98.0 all-reduce.11
